TPU v7x, 512 devices: a whole 4x4x16 slice. The times are simulated.
512 devices in a mesh: chain: 32 (over y, z_lo, core), block: 16 (over z_hi, x).
Axes of the slice: x: 4, y: 4, z: 16 (z_hi: 4, z_lo: 4; z = z_hi * 4 + z_lo), core: 2. Of those that a mesh axis runs over, the one named last changes fastest.
Arguments:
- state: bfloat16 [32, 16, 512, 512], P('chain', 'block'), may hold values from -400 to 400
- left_env: bfloat16 [32, 16, 2, 512, 512], P('chain', 'block'), may hold values from -1 to 5
- right_env: bfloat16 [32, 16, 2, 512, 512], P('chain', 'block'), may hold values from -1 to 5
- precond: float32 [32, 16, 512, 512], P('chain', 'block'), may hold values from 0.2 to 1
- ranks: int32 [32], P('chain'), may hold values from 1024 to 2048
Outputs:
- bond_out: bfloat16 [32, 16, 512, 512], P('chain', 'block')
All inputs are finite; a program needn't handle non-finite values.
Results may differ from a plain program's by a relative error of at most 0.0063.
Values may be sent and summed in bfloat16 or wider, within the bound.
No kernel may reach another device: no remote copies, remote signals or barrier semaphores. Data moves between devices by JAX's collectives and lax.ppermute only.
A program may use at most 64 MiB of HBM per device.

v0:
```python
import math
import jax
import jax.numpy as jnp
from jax import lax
from jax.sharding import Mesh
from jax.sharding import PartitionSpec as P

BLOCK = ("block_0", "block_1")


def from_partner(value, axis, distance):
    mask = 2**distance
    pairs = [(source, source ^ mask) for source in range(lax.axis_size(axis))]
    return lax.ppermute(value, axis, pairs)


def one_axis_at_a_time(x, axes):
    for axis in axes:
        x = lax.psum(x, axis)
    return x


def from_behind(value, axis, steps):
    count = lax.axis_size(axis)
    pairs = [(source, (source + steps) % count) for source in range(count)]
    return lax.ppermute(value, axis, pairs)


def join_halves(gathered, partner, position, bit_number, along):
    lower_half = position >> bit_number & 1 == 0
    first_way = jnp.concatenate([gathered, partner], along)
    second_way = jnp.concatenate([partner, gathered], along)
    return jnp.where(lower_half, first_way, second_way)


def unreverse(gathered, along, levels):
    shape = gathered.shape
    split_shape = shape[:along] + (2,) * levels + (shape[along] // 2**levels,) + shape[along + 1 :]
    order = (
        list(range(along))
        + list(range(along + levels - 1, along - 1, -1))
        + list(range(along + levels, len(split_shape)))
    )
    return gathered.reshape(split_shape).transpose(order).reshape(shape)


def gather_state_rows(gathered, position, levels):
    for level in range(levels):
        partner = from_partner(gathered, BLOCK, level)
        gathered = join_halves(gathered, partner, position, level, 1)
    return gathered


def gather_left_rows(gathered, position, levels):
    for level in range(levels):
        partner = from_partner(gathered, BLOCK, level)
        gathered = join_halves(gathered, partner, position, level, 2)
    return gathered


def gather_right_cols(gathered, position, levels):
    for level in range(levels):
        partner = from_partner(gathered, BLOCK, levels + level)
        gathered = join_halves(gathered, partner, position, levels + level, 1)
    return gathered


def gather_mid_cols(gathered, position, levels):
    level_order = list(range(levels - 1, -1, -1))
    for level in level_order:
        partner = from_partner(gathered, BLOCK, levels + level)
        gathered = join_halves(gathered, partner, position, levels + level, 1)
    gathered = unreverse(gathered, 1, levels)
    return gathered


def mix_weighted(first_tile, second_tile, first_weight, second_weight):
    return (
        first_weight * first_tile.astype(jnp.float32)
        + second_weight * second_tile.astype(jnp.float32)
    ).astype(jnp.bfloat16)


def per_device(state, left_env, right_env, precond, ranks):
    grid_side = math.isqrt(lax.axis_size(BLOCK))
    levels = grid_side.bit_length() - 1
    position = lax.axis_index(BLOCK)
    state_tile = state[0, 0]
    left_tiles = left_env[0, 0]
    right_tiles = right_env[0, 0]
    scaling = precond[0, 0]
    width = state_tile.shape[0]
    order_full = grid_side * width
    state_rows = gather_state_rows(state_tile, position, levels)
    left_rows = gather_left_rows(left_tiles, position, levels)
    right_cols = gather_right_cols(right_tiles, position, levels)
    middle = jnp.einsum(
        "ij,kjl->kil", state_rows, right_cols, preferred_element_type=jnp.float32
    ).astype(jnp.bfloat16)
    middle_cols = gather_mid_cols(middle, position, levels)
    image = jnp.einsum("kij,kjl->il", left_rows, middle_cols, preferred_element_type=jnp.float32)
    state_f = state_tile.astype(jnp.float32)
    row_index = position // grid_side * width + jnp.arange(width, dtype=jnp.int32)
    col_index = position % grid_side * width + jnp.arange(width, dtype=jnp.int32)
    rank_limit = ranks[0]
    keep_mask = ((row_index[:, None] < rank_limit) & (col_index[None, :] < rank_limit)).astype(
        jnp.float32
    )
    total_count = float(order_full * order_full)
    weighted = keep_mask * scaling
    state_sq = state_f * state_f
    cross_term = state_f * image
    moment_terms = (
        jnp.sum(state_sq),
        jnp.sum(cross_term),
        jnp.sum(keep_mask * state_sq),
        jnp.sum(weighted * state_sq),
        jnp.sum(weighted * scaling * state_sq),
        jnp.sum(weighted * cross_term),
        jnp.sum(weighted * scaling * cross_term),
        jnp.sum(weighted * scaling * image * image),
    )
    norm_state, intersection, plain_sq, first_sq, second_sq, first_cross, second_cross, image_sq = (
        one_axis_at_a_time(moment_terms[0], BLOCK),
        one_axis_at_a_time(moment_terms[1], BLOCK),
        one_axis_at_a_time(moment_terms[2], BLOCK),
        one_axis_at_a_time(moment_terms[3], BLOCK),
        one_axis_at_a_time(moment_terms[4], BLOCK),
        one_axis_at_a_time(moment_terms[5], BLOCK),
        one_axis_at_a_time(moment_terms[6], BLOCK),
        one_axis_at_a_time(moment_terms[7], BLOCK),
    )
    energy = intersection / norm_state
    corrected = keep_mask * (state_f - (image - energy * state_f) * scaling)
    square_sum = (
        plain_sq
        + 2.0 * energy * first_sq
        + energy * energy * second_sq
        - 2.0 * first_cross
        - 2.0 * energy * second_cross
        + image_sq
    )
    bond = (corrected / jnp.sqrt(square_sum / total_count + 1e-06)).astype(jnp.bfloat16)
    partner = from_partner(bond, "chain", 0)
    own_pair = mix_weighted(bond, partner, 0.75, 0.25)
    ahead = from_behind(own_pair, "chain", -1)
    crossed = from_partner(ahead, "chain", 0)
    other_pair = from_behind(crossed, "chain", 1)
    result = mix_weighted(own_pair, other_pair, 0.5, 0.5)
    return result[None, None]


def solution(mesh):
    split = Mesh(mesh.devices.reshape(mesh.shape["chain"], 4, 4), ("chain", "block_0", "block_1"))
    placed = (
        P("chain", BLOCK, None, None),
        P("chain", BLOCK, None, None, None),
        P("chain", BLOCK, None, None, None),
        P("chain", BLOCK, None, None),
        P("chain"),
    )
    return jax.shard_map(
        per_device,
        mesh=split,
        in_specs=placed,
        out_specs=P("chain", BLOCK, None, None),
        check_vma=False,
    )
```

profile of v0, /device:TPU:2, one launch (start us, length us, event | category | flops | bytes accessed | tf_op | source)
XLA Modules:
  0.0 672.2 jit_solution(9116957013693709141)
XLA Ops:
  0.0 9.2 %collective-permute-start.2 = (bf16[2,512,512]{2,1,0:T(8,128)(2,1)}, bf16[2,512,512]{2,1,0:T(8,128)(2,1)}, u32[]{:S(2)}, u32[]{:S(2)}) collective-permute-start(bf16[2,512,512]{2,1,0:T(8,128)(2,1)} %bitcast.46), channel_id=1, source_target_pairs={{0,4},{1,5},{2,6},{3,7},{4,0},{5,1},{6,2},{7,3},{8,12},{9,13},{10,... | collective-permute-start | bytes 3145736 | tf_op jit(solution)/shard_map/ppermute | solution.py:14
  9.2 136.1 %collective-permute-done.2 = bf16[2,512,512]{2,1,0:T(8,128)(2,1)} collective-permute-done((bf16[2,512,512]{2,1,0:T(8,128)(2,1)}, bf16[2,512,512]{2,1,0:T(8,128)(2,1)}, u32[]{:S(2)}, u32[]{:S(2)}) %collective-permute-start.2) | collective-permute-done | bytes 1048608 | tf_op jit(solution)/shard_map/ppermute | solution.py:14
  145.3 2.8 maximum_select_fusion.7
  148.2 127.8 %collective-permute-start.3 = (bf16[2,1024,512]{2,1,0:T(8,128)(2,1)S(1)}, bf16[2,1024,512]{2,1,0:T(8,128)(2,1)}, u32[]{:S(2)}, u32[]{:S(2)}) collective-permute-start(bf16[2,1024,512]{2,1,0:T(8,128)(2,1)S(1)} %maximum_select_fusion.7), channel_id=1, source_target_pairs={{0,8},{1,9},{2,10},{3,11},{4,12},{5,13},{6,14},{7,15},{8,0},{9,1},... | collective-permute-start | bytes 6291464 | tf_op jit(solution)/shard_map/ppermute | solution.py:14
  276.0 2.4 collective-permute-start.4
  278.5 12.5 %collective-permute-done.4 = bf16[512,512]{1,0:T(8,128)(2,1)S(1)} collective-permute-done((bf16[512,512]{1,0:T(8,128)(2,1)S(1)}, bf16[512,512]{1,0:T(8,128)(2,1)S(1)}, u32[]{:S(2)}, u32[]{:S(2)}) %collective-permute-start.4) | collective-permute-done | bytes 524320 | tf_op jit(solution)/shard_map/ppermute | solution.py:14
  292.3 4.0 collective-permute-start.5
  296.3 23.2 %collective-permute-done.5 = bf16[512,1024]{1,0:T(8,128)(2,1)} collective-permute-done((bf16[512,1024]{1,0:T(8,128)(2,1)}, bf16[512,1024]{1,0:T(8,128)(2,1)}, u32[]{:S(2)}, u32[]{:S(2)}) %collective-permute-start.5) | collective-permute-done | bytes 1048608 | tf_op jit(solution)/shard_map/ppermute | solution.py:14
  319.6 2.2 collective-permute-done.3
  321.8 5.9 fusion.29
  327.6 12.2 %collective-permute-start.6 = (bf16[2,512,512]{2,1,0:T(8,128)(2,1)S(1)}, bf16[2,512,512]{2,1,0:T(8,128)(2,1)S(1)}, u32[]{:S(2)}, u32[]{:S(2)}) collective-permute-start(bf16[2,512,512]{2,1,0:T(8,128)(2,1)S(1)} %fusion.29), channel_id=1, source_target_pairs={{0,8},{1,9},{2,10},{3,11},{4,12},{5,13},{6,14},{7,15},{8,0},{9,1},... | collective-permute-start | bytes 3145736 | tf_op jit(solution)/shard_map/ppermute | solution.py:14
  339.9 2.4 collective-permute-start
  342.4 19.9 %collective-permute-done.6 = bf16[2,512,512]{2,1,0:T(8,128)(2,1)S(1)} collective-permute-done((bf16[2,512,512]{2,1,0:T(8,128)(2,1)S(1)}, bf16[2,512,512]{2,1,0:T(8,128)(2,1)S(1)}, u32[]{:S(2)}, u32[]{:S(2)}) %collective-permute-start.6) | collective-permute-done | bytes 1048608 | tf_op jit(solution)/shard_map/ppermute | solution.py:14
  362.9 170.4 %collective-permute-start.7 = (bf16[2,1024,512]{2,1,0:T(8,128)(2,1)S(1)}, bf16[2,1024,512]{2,1,0:T(8,128)(2,1)}, u32[]{:S(2)}, u32[]{:S(2)}) collective-permute-start(bf16[2,1024,512]{2,1,0:T(8,128)(2,1)S(1)} %maximum_select_fusion.8), channel_id=1, source_target_pairs={{0,4},{1,5},{2,6},{3,7},{4,0},{5,1},{6,2},{7,3},{8,12},{9,13},{10,... | collective-permute-start | bytes 6291464 | tf_op jit(solution)/shard_map/ppermute | solution.py:14
  535.4 4.0 collective-permute-start.1
  540.1 39.1 %collective-permute-done.7 = bf16[2,1024,512]{2,1,0:T(8,128)(2,1)} collective-permute-done((bf16[2,1024,512]{2,1,0:T(8,128)(2,1)S(1)}, bf16[2,1024,512]{2,1,0:T(8,128)(2,1)}, u32[]{:S(2)}, u32[]{:S(2)}) %collective-permute-start.7) | collective-permute-done | bytes 2097184 | tf_op jit(solution)/shard_map/ppermute | solution.py:14
  579.2 3.3 maximum_select_fusion.4
  582.8 3.5 collective-permute-done.1
  586.3 5.9 multiply_reduce_fusion
  592.1 14.3 %all-reduce.1 = (f32[]{:T(128)}, f32[]{:T(128)}, f32[]{:T(128)}, f32[]{:T(128)}, f32[]{:T(128)}, /*index=5*/f32[]{:T(128)}, f32[]{:T(128)}, f32[]{:T(128)}) all-reduce(f32[]{:T(128)} %get-tuple-element.11, f32[]{:T(128)} %get-tuple-element.10, f32[]{:T(128)} %get-tuple-element.12, ...), channel_id=1, replica_groups=mesh['chain'=32,'block_0'=4,'block_1'=4] {'block_0'}, use_global_device_ids=true, to_apply=%region_7.8 | all-reduce | flops 8 | bytes 64 | tf_op jit(solution)/shard_map/psum | solution.py:19
  606.5 9.3 %all-reduce = (f32[]{:T(128)}, f32[]{:T(128)}, f32[]{:T(128)}, f32[]{:T(128)}, f32[]{:T(128)}, /*index=5*/f32[]{:T(128)}, f32[]{:T(128)}, f32[]{:T(128)}) all-reduce(f32[]{:T(128)} %get-tuple-element.21, f32[]{:T(128)} %get-tuple-element.22, f32[]{:T(128)} %get-tuple-element.23, ...), channel_id=1, replica_groups=mesh['chain'=32,'block_0'=4,'block_1'=4] {'block_1'}, use_global_device_ids=true, to_apply=%region_8.9 | all-reduce | flops 8 | bytes 64 | tf_op jit(solution)/shard_map/psum | solution.py:19
  625.3 20.9 %collective-permute-start.9 = (bf16[512,512]{1,0:T(8,128)(2,1)S(1)}, bf16[512,512]{1,0:T(8,128)(2,1)S(1)}, u32[]{:S(2)}, u32[]{:S(2)}) collective-permute-start(bf16[512,512]{1,0:T(8,128)(2,1)S(1)} %add_convert_fusion), channel_id=1, source_target_pairs={{0,496},{16,0},{32,16},{48,32},{64,48},{80,64},{96,80},{112,96},{1... | collective-permute-start | bytes 1572872 | tf_op jit(solution)/shard_map/ppermute | solution.py:26
  646.2 6.7 collective-permute-done.9
  658.7 12.5 %collective-permute-done.11 = bf16[512,512]{1,0:T(8,128)(2,1)S(1)} collective-permute-done((bf16[512,512]{1,0:T(8,128)(2,1)S(1)}, bf16[512,512]{1,0:T(8,128)(2,1)S(1)}, u32[]{:S(2)}, u32[]{:S(2)}) %collective-permute-start.11) | collective-permute-done | bytes 524320 | tf_op jit(solution)/shard_map/ppermute | solution.py:26
  (20 shorter events, 15.4 us)
Async XLA Ops:
  0.0 276.0 %copy-start = (bf16[1,1,512,512]{3,2,1,0:T(8,128)(2,1)S(1)}, bf16[1,1,512,512]{3,2,1,0:T(8,128)(2,1)}, u32[]{:S(2)}) copy-start(bf16[1,1,512,512]{3,2,1,0:T(8,128)(2,1)} %param.5) | copy-start | bytes 1572868
  0.0 145.3 %collective-permute-start.2 = (bf16[2,512,512]{2,1,0:T(8,128)(2,1)}, bf16[2,512,512]{2,1,0:T(8,128)(2,1)}, u32[]{:S(2)}, u32[]{:S(2)}) collective-permute-start(bf16[2,512,512]{2,1,0:T(8,128)(2,1)} %bitcast.46), channel_id=1, source_target_pairs={{0,4},{1,5},{2,6},{3,7},{4,0},{5,1},{6,2},{7,3},{8,12},{9,13},{10,... | collective-permute-start | bytes 3145736 | tf_op jit(solution)/shard_map/ppermute | solution.py:14
  148.2 173.6 %collective-permute-start.3 = (bf16[2,1024,512]{2,1,0:T(8,128)(2,1)S(1)}, bf16[2,1024,512]{2,1,0:T(8,128)(2,1)}, u32[]{:S(2)}, u32[]{:S(2)}) collective-permute-start(bf16[2,1024,512]{2,1,0:T(8,128)(2,1)S(1)} %maximum_select_fusion.7), channel_id=1, source_target_pairs={{0,8},{1,9},{2,10},{3,11},{4,12},{5,13},{6,14},{7,15},{8,0},{9,1},... | collective-permute-start | bytes 6291464 | tf_op jit(solution)/shard_map/ppermute | solution.py:14
  276.0 15.0 %collective-permute-start.4 = (bf16[512,512]{1,0:T(8,128)(2,1)S(1)}, bf16[512,512]{1,0:T(8,128)(2,1)S(1)}, u32[]{:S(2)}, u32[]{:S(2)}) collective-permute-start(bf16[512,512]{1,0:T(8,128)(2,1)S(1)} %bitcast.44), channel_id=1, source_target_pairs={{0,1},{1,0},{2,3},{3,2},{4,5},{5,4},{6,7},{7,6},{8,9},{9,8},{10,11... | collective-permute-start | bytes 1572872 | tf_op jit(solution)/shard_map/ppermute | solution.py:14
  292.3 27.3 %collective-permute-start.5 = (bf16[512,1024]{1,0:T(8,128)(2,1)}, bf16[512,1024]{1,0:T(8,128)(2,1)}, u32[]{:S(2)}, u32[]{:S(2)}) collective-permute-start(bf16[512,1024]{1,0:T(8,128)(2,1)} %maximum_select_fusion.15), channel_id=1, source_target_pairs={{0,2},{1,3},{2,0},{3,1},{4,6},{5,7},{6,4},{7,5},{8,10},{9,11},{10,... | collective-permute-start | bytes 3145736 | tf_op jit(solution)/shard_map/ppermute | solution.py:14
  296.3 43.6 %copy-start.1 = (bf16[1,1,2,512,512]{4,3,2,1,0:T(8,128)(2,1)S(1)}, bf16[1,1,2,512,512]{4,3,2,1,0:T(8,128)(2,1)}, u32[]{:S(2)}) copy-start(bf16[1,1,2,512,512]{4,3,2,1,0:T(8,128)(2,1)} %param.6) | copy-start | bytes 3145732
  327.6 34.6 %collective-permute-start.6 = (bf16[2,512,512]{2,1,0:T(8,128)(2,1)S(1)}, bf16[2,512,512]{2,1,0:T(8,128)(2,1)S(1)}, u32[]{:S(2)}, u32[]{:S(2)}) collective-permute-start(bf16[2,512,512]{2,1,0:T(8,128)(2,1)S(1)} %fusion.29), channel_id=1, source_target_pairs={{0,8},{1,9},{2,10},{3,11},{4,12},{5,13},{6,14},{7,15},{8,0},{9,1},... | collective-permute-start | bytes 3145736 | tf_op jit(solution)/shard_map/ppermute | solution.py:14
  339.9 193.5 %collective-permute-start = (bf16[2,512,512]{2,1,0:T(8,128)(2,1)S(1)}, bf16[2,512,512]{2,1,0:T(8,128)(2,1)S(1)}, u32[]{:S(2)}, u32[]{:S(2)}) collective-permute-start(bf16[2,512,512]{2,1,0:T(8,128)(2,1)S(1)} %bitcast.48), channel_id=1, source_target_pairs={{0,1},{1,0},{2,3},{3,2},{4,5},{5,4},{6,7},{7,6},{8,9},{9,8},{10,11... | collective-permute-start | bytes 3145736 | tf_op jit(solution)/shard_map/ppermute | solution.py:14
  362.9 216.2 %collective-permute-start.7 = (bf16[2,1024,512]{2,1,0:T(8,128)(2,1)S(1)}, bf16[2,1024,512]{2,1,0:T(8,128)(2,1)}, u32[]{:S(2)}, u32[]{:S(2)}) collective-permute-start(bf16[2,1024,512]{2,1,0:T(8,128)(2,1)S(1)} %maximum_select_fusion.8), channel_id=1, source_target_pairs={{0,4},{1,5},{2,6},{3,7},{4,0},{5,1},{6,2},{7,3},{8,12},{9,13},{10,... | collective-permute-start | bytes 6291464 | tf_op jit(solution)/shard_map/ppermute | solution.py:14
  535.4 50.9 %collective-permute-start.1 = (bf16[2,512,1024]{2,1,0:T(8,128)(2,1)}, bf16[2,512,1024]{2,1,0:T(8,128)(2,1)}, u32[]{:S(2)}, u32[]{:S(2)}) collective-permute-start(bf16[2,512,1024]{2,1,0:T(8,128)(2,1)} %maximum_select_fusion.5), channel_id=1, source_target_pairs={{0,2},{1,3},{2,0},{3,1},{4,6},{5,7},{6,4},{7,5},{8,10},{9,11},{10,... | collective-permute-start | bytes 6291464 | tf_op jit(solution)/shard_map/ppermute | solution.py:14
  582.5 3.8 copy-start.2
  621.3 3.8 collective-permute-start.8
  625.3 27.6 %collective-permute-start.9 = (bf16[512,512]{1,0:T(8,128)(2,1)S(1)}, bf16[512,512]{1,0:T(8,128)(2,1)S(1)}, u32[]{:S(2)}, u32[]{:S(2)}) collective-permute-start(bf16[512,512]{1,0:T(8,128)(2,1)S(1)} %add_convert_fusion), channel_id=1, source_target_pairs={{0,496},{16,0},{32,16},{48,32},{64,48},{80,64},{96,80},{112,96},{1... | collective-permute-start | bytes 1572872 | tf_op jit(solution)/shard_map/ppermute | solution.py:26
  652.9 3.8 collective-permute-start.10
  656.7 14.6 %collective-permute-start.11 = (bf16[512,512]{1,0:T(8,128)(2,1)S(1)}, bf16[512,512]{1,0:T(8,128)(2,1)S(1)}, u32[]{:S(2)}, u32[]{:S(2)}) collective-permute-start(bf16[512,512]{1,0:T(8,128)(2,1)S(1)} %collective-permute-done.10), channel_id=1, source_target_pairs={{0,16},{16,32},{32,48},{48,64},{64,80},{80,96},{96,112},{112,128},... | collective-permute-start | bytes 1572872 | tf_op jit(solution)/shard_map/ppermute | solution.py:26
where the time goes:
time: 673 us; the launch traced here: 672 us
  starting transfers between devices  359 us (53%)
  waiting for transfers between devices  259 us (38%)
  blocking collectives  23.6 us (4%)
  matrix products  11.7 us (2%)
  other arithmetic  11.6 us (2%)
    ppermute x10, starting transfers between devices, from_partner(): return lax.ppermute(value, axis, pairs)  336 us
    ppermute x10, waiting for transfers between devices, from_partner(): return lax.ppermute(value, axis, pairs)  240 us
    psum x2, blocking collectives, one_axis_at_a_time(): x = lax.psum(x, axis)  23.6 us
    ppermute x2, starting transfers between devices, from_behind(): return lax.ppermute(value, axis, pairs)  23 us
    ppermute x2, waiting for transfers between devices, from_behind(): return lax.ppermute(value, axis, pairs)  19.2 us
  transfers between devices with their start and end apart: 12, of which 11 were waited for; matrix products, arithmetic and copies ran while one was open for 1% of the time, Pallas kernels for 0%

commit v1 on v0

--- a/solution.py
+++ b/solution.py
@@ -16,7 +16,7 @@
 
 def one_axis_at_a_time(x, axes):
     for axis in axes:
-        x = lax.psum(x, axis)
+        x = jnp.sum(lax.all_gather(x, axis), axis=0)
     return x
 
 

time: 673 us -> 729 us (1.083)
  local copies, waits for them, and re-layouts: 0.29 us -> 48.5 us
  other arithmetic: 11.6 us -> 21.4 us
    unnamed x6 -> x40, local copies, waits for them, and re-layouts: 0.02 us -> 48.2 us
    psum x2 -> x0, blocking collectives: 23.6 us -> none  [one_axis_at_a_time(): x = lax.psum(x, axis)]
    unnamed x0 -> x2, blocking collectives: none -> 22.5 us
    reduce_sum x0 -> x16, other arithmetic: none -> 9.74 us  [one_axis_at_a_time(): x = jnp.sum(lax.all_gather(x, axis), axis=0)]
where the time goes in v1:
time: 729 us; the launch traced here: 728 us
  starting transfers between devices  359 us (49%)
  waiting for transfers between devices  258 us (35%)
  local copies, waits for them, and re-layouts  48.5 us (7%)
  blocking collectives  22.5 us (3%)
  other arithmetic  21.4 us (3%)
  matrix products  11.8 us (2%)
    ppermute x10, starting transfers between devices, from_partner(): return lax.ppermute(value, axis, pairs)  337 us
    ppermute x10, waiting for transfers between devices, from_partner(): return lax.ppermute(value, axis, pairs)  239 us
    unnamed x40, local copies, waits for them, and re-layouts  48.2 us
    ppermute x2, starting transfers between devices, from_behind(): return lax.ppermute(value, axis, pairs)  22.9 us
    unnamed x2, blocking collectives  22.5 us
    ppermute x2, waiting for transfers between devices, from_behind(): return lax.ppermute(value, axis, pairs)  19.2 us
  transfers between devices with their start and end apart: 12, of which 11 were waited for; matrix products, arithmetic and copies ran while one was open for 1% of the time, Pallas kernels for 0%

profile of v1, /device:TPU:2, one launch (start us, length us, event | category | flops | bytes accessed | tf_op | source)
XLA Modules:
  0.0 728.1 jit_solution(13705474302662155650)
XLA Ops:
  0.0 9.2 %collective-permute-start.2 = (bf16[2,512,512]{2,1,0:T(8,128)(2,1)}, bf16[2,512,512]{2,1,0:T(8,128)(2,1)}, u32[]{:S(2)}, u32[]{:S(2)}) collective-permute-start(bf16[2,512,512]{2,1,0:T(8,128)(2,1)} %bitcast.64), channel_id=1, source_target_pairs={{0,4},{1,5},{2,6},{3,7},{4,0},{5,1},{6,2},{7,3},{8,12},{9,13},{10,... | collective-permute-start | bytes 3145736 | tf_op jit(solution)/shard_map/ppermute | solution.py:14
  9.2 136.1 %collective-permute-done.2 = bf16[2,512,512]{2,1,0:T(8,128)(2,1)} collective-permute-done((bf16[2,512,512]{2,1,0:T(8,128)(2,1)}, bf16[2,512,512]{2,1,0:T(8,128)(2,1)}, u32[]{:S(2)}, u32[]{:S(2)}) %collective-permute-start.2) | collective-permute-done | bytes 1048608 | tf_op jit(solution)/shard_map/ppermute | solution.py:14
  145.3 2.8 maximum_select_fusion.7
  148.2 127.8 %collective-permute-start.3 = (bf16[2,1024,512]{2,1,0:T(8,128)(2,1)S(1)}, bf16[2,1024,512]{2,1,0:T(8,128)(2,1)}, u32[]{:S(2)}, u32[]{:S(2)}) collective-permute-start(bf16[2,1024,512]{2,1,0:T(8,128)(2,1)S(1)} %maximum_select_fusion.7), channel_id=1, source_target_pairs={{0,8},{1,9},{2,10},{3,11},{4,12},{5,13},{6,14},{7,15},{8,0},{9,1},... | collective-permute-start | bytes 6291464 | tf_op jit(solution)/shard_map/ppermute | solution.py:14
  278.5 12.5 %collective-permute-done.4 = bf16[512,512]{1,0:T(8,128)(2,1)S(1)} collective-permute-done((bf16[512,512]{1,0:T(8,128)(2,1)S(1)}, bf16[512,512]{1,0:T(8,128)(2,1)S(1)}, u32[]{:S(2)}, u32[]{:S(2)}) %collective-permute-start.4) | collective-permute-done | bytes 524320 | tf_op jit(solution)/shard_map/ppermute | solution.py:14
  292.3 4.0 collective-permute-start.5
  296.3 23.2 %collective-permute-done.5 = bf16[512,1024]{1,0:T(8,128)(2,1)} collective-permute-done((bf16[512,1024]{1,0:T(8,128)(2,1)}, bf16[512,1024]{1,0:T(8,128)(2,1)}, u32[]{:S(2)}, u32[]{:S(2)}) %collective-permute-start.5) | collective-permute-done | bytes 1048608 | tf_op jit(solution)/shard_map/ppermute | solution.py:14
  321.8 5.9 fusion.29
  327.6 12.2 %collective-permute-start.6 = (bf16[2,512,512]{2,1,0:T(8,128)(2,1)S(1)}, bf16[2,512,512]{2,1,0:T(8,128)(2,1)S(1)}, u32[]{:S(2)}, u32[]{:S(2)}) collective-permute-start(bf16[2,512,512]{2,1,0:T(8,128)(2,1)S(1)} %fusion.29), channel_id=1, source_target_pairs={{0,8},{1,9},{2,10},{3,11},{4,12},{5,13},{6,14},{7,15},{8,0},{9,1},... | collective-permute-start | bytes 3145736 | tf_op jit(solution)/shard_map/ppermute | solution.py:14
  342.4 19.9 %collective-permute-done.6 = bf16[2,512,512]{2,1,0:T(8,128)(2,1)S(1)} collective-permute-done((bf16[2,512,512]{2,1,0:T(8,128)(2,1)S(1)}, bf16[2,512,512]{2,1,0:T(8,128)(2,1)S(1)}, u32[]{:S(2)}, u32[]{:S(2)}) %collective-permute-start.6) | collective-permute-done | bytes 1048608 | tf_op jit(solution)/shard_map/ppermute | solution.py:14
  362.9 170.5 %collective-permute-start.7 = (bf16[2,1024,512]{2,1,0:T(8,128)(2,1)S(1)}, bf16[2,1024,512]{2,1,0:T(8,128)(2,1)}, u32[]{:S(2)}, u32[]{:S(2)}) collective-permute-start(bf16[2,1024,512]{2,1,0:T(8,128)(2,1)S(1)} %maximum_select_fusion.8), channel_id=1, source_target_pairs={{0,4},{1,5},{2,6},{3,7},{4,0},{5,1},{6,2},{7,3},{8,12},{9,13},{10,... | collective-permute-start | bytes 6291464 | tf_op jit(solution)/shard_map/ppermute | solution.py:14
  535.4 4.0 collective-permute-start.1
  541.4 37.9 %collective-permute-done.7 = bf16[2,1024,512]{2,1,0:T(8,128)(2,1)} collective-permute-done((bf16[2,1024,512]{2,1,0:T(8,128)(2,1)S(1)}, bf16[2,1024,512]{2,1,0:T(8,128)(2,1)}, u32[]{:S(2)}, u32[]{:S(2)}) %collective-permute-start.7) | collective-permute-done | bytes 2097184 | tf_op jit(solution)/shard_map/ppermute | solution.py:14
  579.3 3.3 maximum_select_fusion.4
  582.9 3.5 collective-permute-done.1
  586.4 6.0 multiply_reduce_fusion
  616.0 13.8 %all-reduce.17 = (f32[4]{0:T(128)S(1)}, f32[4]{0:T(128)S(1)}, f32[4]{0:T(128)S(1)}, f32[4]{0:T(128)S(1)}, f32[4]{0:T(128)S(1)}, /*index=5*/f32[4]{0:T(128)S(1)}, f32[4]{0:T(128)S(1)}, f32[4]{0:T(128)S(1)}) all-reduce(f32[4]{0:T(128)} %dynamic-update-slice.4, ...), channel_id=1, replica_groups=mesh['chain'=32,'block_0'=4,'block_1'=4] {'block_0'}, use_global_device_ids=true, to_apply=%add.4 | all-reduce | flops 32 | bytes 256
  636.6 2.7 dynamic-update-slice.15
  640.5 2.6 dynamic-update-slice.3
  651.5 2.7 dynamic-update-slice.1
  657.9 8.7 %all-reduce.16 = (f32[4]{0:T(128)S(1)}, f32[4]{0:T(128)S(1)}, f32[4]{0:T(128)S(1)}, f32[4]{0:T(128)S(1)}, f32[4]{0:T(128)S(1)}, /*index=5*/f32[4]{0:T(128)S(1)}, f32[4]{0:T(128)S(1)}, f32[4]{0:T(128)S(1)}) all-reduce(f32[4]{0:T(128)} %dynamic-update-slice.5, ...), channel_id=1, replica_groups=mesh['chain'=32,'block_0'=4,'block_1'=4] {'block_1'}, use_global_device_ids=true, to_apply=%add.5 | all-reduce | flops 32 | bytes 256
  681.2 20.9 %collective-permute-start.9 = (bf16[512,512]{1,0:T(8,128)(2,1)S(1)}, bf16[512,512]{1,0:T(8,128)(2,1)S(1)}, u32[]{:S(2)}, u32[]{:S(2)}) collective-permute-start(bf16[512,512]{1,0:T(8,128)(2,1)S(1)} %add_convert_fusion), channel_id=1, source_target_pairs={{0,496},{16,0},{32,16},{48,32},{64,48},{80,64},{96,80},{112,96},{1... | collective-permute-start | bytes 1572872 | tf_op jit(solution)/shard_map/ppermute | solution.py:26
  702.1 6.7 collective-permute-done.9
  714.6 12.5 %collective-permute-done.11 = bf16[512,512]{1,0:T(8,128)(2,1)S(1)} collective-permute-done((bf16[512,512]{1,0:T(8,128)(2,1)S(1)}, bf16[512,512]{1,0:T(8,128)(2,1)S(1)}, u32[]{:S(2)}, u32[]{:S(2)}) %collective-permute-start.11) | collective-permute-done | bytes 524320 | tf_op jit(solution)/shard_map/ppermute | solution.py:26
  (70 shorter events, 72.5 us)
Async XLA Ops:
  0.0 276.0 %copy-start = (bf16[1,1,512,512]{3,2,1,0:T(8,128)(2,1)S(1)}, bf16[1,1,512,512]{3,2,1,0:T(8,128)(2,1)}, u32[]{:S(2)}) copy-start(bf16[1,1,512,512]{3,2,1,0:T(8,128)(2,1)} %param.5) | copy-start | bytes 1572868
  0.0 145.3 %collective-permute-start.2 = (bf16[2,512,512]{2,1,0:T(8,128)(2,1)}, bf16[2,512,512]{2,1,0:T(8,128)(2,1)}, u32[]{:S(2)}, u32[]{:S(2)}) collective-permute-start(bf16[2,512,512]{2,1,0:T(8,128)(2,1)} %bitcast.64), channel_id=1, source_target_pairs={{0,4},{1,5},{2,6},{3,7},{4,0},{5,1},{6,2},{7,3},{8,12},{9,13},{10,... | collective-permute-start | bytes 3145736 | tf_op jit(solution)/shard_map/ppermute | solution.py:14
  148.2 173.6 %collective-permute-start.3 = (bf16[2,1024,512]{2,1,0:T(8,128)(2,1)S(1)}, bf16[2,1024,512]{2,1,0:T(8,128)(2,1)}, u32[]{:S(2)}, u32[]{:S(2)}) collective-permute-start(bf16[2,1024,512]{2,1,0:T(8,128)(2,1)S(1)} %maximum_select_fusion.7), channel_id=1, source_target_pairs={{0,8},{1,9},{2,10},{3,11},{4,12},{5,13},{6,14},{7,15},{8,0},{9,1},... | collective-permute-start | bytes 6291464 | tf_op jit(solution)/shard_map/ppermute | solution.py:14
  276.0 15.0 %collective-permute-start.4 = (bf16[512,512]{1,0:T(8,128)(2,1)S(1)}, bf16[512,512]{1,0:T(8,128)(2,1)S(1)}, u32[]{:S(2)}, u32[]{:S(2)}) collective-permute-start(bf16[512,512]{1,0:T(8,128)(2,1)S(1)} %bitcast.62), channel_id=1, source_target_pairs={{0,1},{1,0},{2,3},{3,2},{4,5},{5,4},{6,7},{7,6},{8,9},{9,8},{10,11... | collective-permute-start | bytes 1572872 | tf_op jit(solution)/shard_map/ppermute | solution.py:14
  292.3 27.3 %collective-permute-start.5 = (bf16[512,1024]{1,0:T(8,128)(2,1)}, bf16[512,1024]{1,0:T(8,128)(2,1)}, u32[]{:S(2)}, u32[]{:S(2)}) collective-permute-start(bf16[512,1024]{1,0:T(8,128)(2,1)} %maximum_select_fusion.15), channel_id=1, source_target_pairs={{0,2},{1,3},{2,0},{3,1},{4,6},{5,7},{6,4},{7,5},{8,10},{9,11},{10,... | collective-permute-start | bytes 3145736 | tf_op jit(solution)/shard_map/ppermute | solution.py:14
  296.3 43.6 %copy-start.1 = (bf16[1,1,2,512,512]{4,3,2,1,0:T(8,128)(2,1)S(1)}, bf16[1,1,2,512,512]{4,3,2,1,0:T(8,128)(2,1)}, u32[]{:S(2)}) copy-start(bf16[1,1,2,512,512]{4,3,2,1,0:T(8,128)(2,1)} %param.6) | copy-start | bytes 3145732
  327.6 34.6 %collective-permute-start.6 = (bf16[2,512,512]{2,1,0:T(8,128)(2,1)S(1)}, bf16[2,512,512]{2,1,0:T(8,128)(2,1)S(1)}, u32[]{:S(2)}, u32[]{:S(2)}) collective-permute-start(bf16[2,512,512]{2,1,0:T(8,128)(2,1)S(1)} %fusion.29), channel_id=1, source_target_pairs={{0,8},{1,9},{2,10},{3,11},{4,12},{5,13},{6,14},{7,15},{8,0},{9,1},... | collective-permute-start | bytes 3145736 | tf_op jit(solution)/shard_map/ppermute | solution.py:14
  339.9 193.5 %collective-permute-start = (bf16[2,512,512]{2,1,0:T(8,128)(2,1)S(1)}, bf16[2,512,512]{2,1,0:T(8,128)(2,1)S(1)}, u32[]{:S(2)}, u32[]{:S(2)}) collective-permute-start(bf16[2,512,512]{2,1,0:T(8,128)(2,1)S(1)} %bitcast.66), channel_id=1, source_target_pairs={{0,1},{1,0},{2,3},{3,2},{4,5},{5,4},{6,7},{7,6},{8,9},{9,8},{10,11... | collective-permute-start | bytes 3145736 | tf_op jit(solution)/shard_map/ppermute | solution.py:14
  362.9 216.4 %collective-permute-start.7 = (bf16[2,1024,512]{2,1,0:T(8,128)(2,1)S(1)}, bf16[2,1024,512]{2,1,0:T(8,128)(2,1)}, u32[]{:S(2)}, u32[]{:S(2)}) collective-permute-start(bf16[2,1024,512]{2,1,0:T(8,128)(2,1)S(1)} %maximum_select_fusion.8), channel_id=1, source_target_pairs={{0,4},{1,5},{2,6},{3,7},{4,0},{5,1},{6,2},{7,3},{8,12},{9,13},{10,... | collective-permute-start | bytes 6291464 | tf_op jit(solution)/shard_map/ppermute | solution.py:14
  535.4 51.0 %collective-permute-start.1 = (bf16[2,512,1024]{2,1,0:T(8,128)(2,1)}, bf16[2,512,1024]{2,1,0:T(8,128)(2,1)}, u32[]{:S(2)}, u32[]{:S(2)}) collective-permute-start(bf16[2,512,1024]{2,1,0:T(8,128)(2,1)} %maximum_select_fusion.5), channel_id=1, source_target_pairs={{0,2},{1,3},{2,0},{3,1},{4,6},{5,7},{6,4},{7,5},{8,10},{9,11},{10,... | collective-permute-start | bytes 6291464 | tf_op jit(solution)/shard_map/ppermute | solution.py:14
  582.6 3.8 copy-start.2
  677.2 3.8 collective-permute-start.8
  681.2 27.6 %collective-permute-start.9 = (bf16[512,512]{1,0:T(8,128)(2,1)S(1)}, bf16[512,512]{1,0:T(8,128)(2,1)S(1)}, u32[]{:S(2)}, u32[]{:S(2)}) collective-permute-start(bf16[512,512]{1,0:T(8,128)(2,1)S(1)} %add_convert_fusion), channel_id=1, source_target_pairs={{0,496},{16,0},{32,16},{48,32},{64,48},{80,64},{96,80},{112,96},{1... | collective-permute-start | bytes 1572872 | tf_op jit(solution)/shard_map/ppermute | solution.py:26
  708.8 3.8 collective-permute-start.10
  712.6 14.6 %collective-permute-start.11 = (bf16[512,512]{1,0:T(8,128)(2,1)S(1)}, bf16[512,512]{1,0:T(8,128)(2,1)S(1)}, u32[]{:S(2)}, u32[]{:S(2)}) collective-permute-start(bf16[512,512]{1,0:T(8,128)(2,1)S(1)} %collective-permute-done.10), channel_id=1, source_target_pairs={{0,16},{16,32},{32,48},{48,64},{64,80},{80,96},{96,112},{112,128},... | collective-permute-start | bytes 1572872 | tf_op jit(solution)/shard_map/ppermute | solution.py:26
